TPU v7x, 32 devices: a whole 2x2x4 slice. The times are simulated.
32 devices in a mesh: grp: 2 (over x), freq: 16 (over z, y, core).
Axes of the slice: x: 2, y: 2, z: 4, core: 2. Of those that a mesh axis runs over, the one named last changes fastest.
Arguments:
- start_field: bfloat16 [512, 384, 512], P(('grp', 'freq')), parts along dimension 0, may hold values from -2.390625 to 2.390625
- recorded: bfloat16 [32, 384, 4, 128], P(('grp', 'freq')), parts along dimension 0, may hold values from -6 to 6
- multiples: bfloat16 [32, 4, 3, 64, 128], P(('grp', 'freq')), parts along dimension 0, may hold values from -0.3125 to 0.3125
- block_index: int32 [4, 3], replicated, may hold values from 0 to 3, all different within a row
- radius: int32 [512, 384], P(('grp', 'freq')), parts along dimension 0, may hold values from 0 to 4
Outputs:
- field: float32 [512, 384, 512], P(('grp', 'freq')), parts along dimension 0
- residual: float32 [32, 384, 4, 128], P(('grp', 'freq')), parts along dimension 0
There are 2 independent parts, one for each index of `grp`. A program takes and returns all parts, laid end to end along the dimension named above; an argument that names none is the same for every part. Nothing has to cross between parts.
Inputs may be any that keep to these rules, and one draw needn't show every extreme that they name: `block_index`: each row names 3 different source blocks, and every block is named by some row.
All inputs are finite; a program needn't handle non-finite values.
Results may differ from a plain program's by a relative error of at most 0.004.
Values may be sent and summed in bfloat16 or wider, within the bound.
A program may use at most 64 MiB of HBM per device.

v0:
```python
import functools
import math

import jax
import jax.numpy as jnp
import numpy as np
from jax import lax
from jax.experimental import pallas as pl
from jax.experimental.pallas import tpu as pltpu
from jax.sharding import PartitionSpec as P

NB = 4
BS = 64
BANDS = 3
RADIUS = 4

step_size = 0.5
shrinkage = 0.05

BF16 = jnp.bfloat16
F32 = jnp.float32


def dft_table(freq_count, samples):
    phases = (np.arange(samples)[:, None] * (np.arange(freq_count) + 1)[None, :]) % samples
    angles = phases.astype(np.float64) * (2.0 * math.pi / samples)
    stacked = np.stack([np.cos(angles), -np.sin(angles)], axis=-1)
    return (stacked.reshape(samples, 2 * freq_count) / math.sqrt(samples)).astype(np.float32)


def halves(table):
    high = jnp.asarray(table).astype(BF16)
    low = (jnp.asarray(table) - high.astype(F32)).astype(BF16)
    return high, low


def soft(update):
    return update - jnp.clip(update, -shrinkage, shrinkage)


def nt_dot(a, b):
    return lax.dot_general(a, b, (((1,), (1,)), ((), ())), preferred_element_type=F32)


def tn_dot(a, b):
    return lax.dot_general(a, b, (((0,), (0,)), ((), ())), preferred_element_type=F32)


def build_operator(block_ref, multiples_ref, inner, local_src):
    parts = BS // local_src
    for f in range(multiples_ref.shape[0]):
        for j in range(NB):
            terms = [multiples_ref[f, j, b].astype(F32) for b in range(BANDS)]
            for m in range(NB):
                block = None
                for b in range(BANDS):
                    term = terms[b] * jnp.where(block_ref[j, b] == m, 1.0, 0.0)
                    block = term if block is None else block + term
                turned = jnp.concatenate([-block[:, BS:], block[:, :BS]], axis=1)
                for q in range(parts):
                    for c, half in enumerate((block, turned)):
                        row = ((m * parts + q) * 2 + c) * local_src
                        piece = half[q * local_src : (q + 1) * local_src]
                        inner[f, row : row + local_src, j * 2 * BS : (j + 1) * 2 * BS] = piece.astype(BF16)


def sweeps_kernel(
    devices, chunks, width,
    block_hbm, start_hbm, recorded_hbm, multiples_hbm, radius_hbm, analysis_hbm, synthesis_hbm,
    field_ref, last_ref, residual_ref,
    field, wide, flat, near, spans, given, inner, out_slabs, in_slabs, back_slabs, edge_slabs, rim_out, rim_in,
    block_ref, recorded_ref, multiples_ref, radius_ref, analysis_ref, synthesis_ref,
    load_sem, send_sem, recv_sem, rim_send, rim_recv, table_sem,
):
    me = lax.axis_index("freq")
    local_src = start_hbm.shape[0]
    local_freq = multiples_hbm.shape[0]
    rows = analysis_ref.shape[0] // 2
    block_cols = 2 * BS

    def load(c):
        return pltpu.make_async_copy(start_hbm.at[:, pl.ds(c * width, width), :], field.at[c], load_sem.at[c])

    load(0).start()
    tables = [
        pltpu.make_async_copy(source, target, table_sem.at[n])
        for n, (source, target) in enumerate(
            (
                (analysis_hbm, analysis_ref),
                (block_hbm, block_ref),
                (multiples_hbm, multiples_ref),
                (radius_hbm, radius_ref),
                (recorded_hbm, recorded_ref),
                (synthesis_hbm, synthesis_ref),
            )
        )
    ]
    tables[0].start()
    for c in range(1, chunks):
        load(c).start()
    for table in tables[1:]:
        table.start()
    barrier = pltpu.get_barrier_semaphore()
    for shift in range(1, devices):
        pl.semaphore_signal(
            barrier, inc=1, device_id={"freq": lax.rem(me + shift, devices)}, device_id_type=pl.DeviceIdType.MESH
        )

    def exchange(phase, c, sources, targets):
        slot = phase * chunks + c
        place = (phase // 2) * chunks + c

        def send(step, carry):
            peer = lax.rem(me + step, devices)
            pltpu.make_async_remote_copy(
                src_ref=sources.at[place, peer],
                dst_ref=targets.at[place, me],
                send_sem=send_sem.at[slot],
                recv_sem=recv_sem.at[slot],
                device_id={"freq": peer},
                device_id_type=pl.DeviceIdType.MESH,
            ).start()
            return carry

        lax.fori_loop(1, devices, send, 0)
        targets[place, me] = sources[place, me]

    def await_all(phase, c, refs, sems):
        whole = refs.at[(phase // 2) * chunks + c, pl.ds(0, devices - 1)]
        pltpu.make_async_copy(whole, whole, sems.at[phase * chunks + c]).wait()

    def rim(place, side):
        return pltpu.make_async_remote_copy(
            src_ref=rim_out.at[place, side],
            dst_ref=rim_in.at[place, side],
            send_sem=rim_send.at[place, side],
            recv_sem=rim_recv.at[place, side],
            device_id={"freq": lax.rem(me + (1 if side == 0 else devices - 1), devices)},
            device_id_type=pl.DeviceIdType.MESH,
        )

    sends = (me < devices - 1, me > 0)
    gets = (me > 0, me < devices - 1)

    def analyse(s, samples):
        both = nt_dot(analysis_ref[...], samples)
        wide[pl.ds(s, rows, stride=local_src), :] = both[:rows] + both[rows:]

    def ship(sweep, c):
        slabs = wide[...].reshape(devices, local_freq * 2 * local_src, width)
        out_slabs[sweep * chunks + c] = slabs.astype(BF16)
        if sweep == 0 and c == 0:
            pl.semaphore_wait(barrier, devices - 1)
        exchange(2 * sweep, c, out_slabs, in_slabs)

    def own(sweep, c):
        await_all(2 * sweep, c, in_slabs, recv_sem)
        arrived = in_slabs[sweep * chunks + c].astype(F32)
        backs = []
        for f in range(local_freq):
            part = arrived[:, f * 2 * local_src : (f + 1) * 2 * local_src]
            owned = part.reshape(devices * 2 * local_src, width).T.astype(BF16)
            predicted = jnp.dot(owned, inner[f], preferred_element_type=F32)
            given[...] = recorded_ref[f, pl.ds(c * width * NB, width * NB), :].astype(F32)
            narrow = []
            for j in range(NB):
                left = given[pl.ds(j, width, stride=NB), :] - predicted[:, j * block_cols : (j + 1) * block_cols]
                if sweep == 1:
                    residual_ref[f, pl.ds(c * width * NB + j, width, stride=NB), :] = left
                narrow.append(left.astype(BF16))
            back = nt_dot(inner[f], jnp.concatenate(narrow, axis=1))
            backs.append(back.reshape(devices, 2 * local_src, width))
        back = backs[0] if local_freq == 1 else jnp.concatenate(backs, axis=1)
        back_slabs[sweep * chunks + c] = back.astype(BF16)
        exchange(2 * sweep + 1, c, back_slabs, edge_slabs)

    def trace_side(sweep, c):
        place = sweep * chunks + c
        await_all(2 * sweep + 1, c, edge_slabs, recv_sem)
        flat[...] = edge_slabs[place].astype(F32).reshape(rows * local_src, width)
        for s in range(local_src):
            near[RADIUS + s] = flat[pl.ds(s, rows, stride=local_src), :]
        rim_out[place, 0] = near[local_src : local_src + RADIUS].astype(BF16)
        rim_out[place, 1] = near[RADIUS : 2 * RADIUS].astype(BF16)
        for side in range(2):

            @pl.when(sends[side])
            def _():
                rim(place, side).start()

        span_lanes = pl.ds(c * width, width)

        def source(s, carry):
            span = spans[s, :, span_lanes]
            box = near[s + RADIUS]
            smoothed = box
            for offset in range(1, RADIUS + 1):
                box = box + (near[s + RADIUS + offset] + near[s + RADIUS - offset])
                smoothed = jnp.where(span >= offset, box, smoothed)
            smoothed = smoothed * (1.0 / (2.0 * span.astype(F32) + 1.0))
            high = smoothed.astype(BF16)
            low = (smoothed - high.astype(F32)).astype(BF16)
            stack = jnp.concatenate([high, low, high], axis=0)
            if sweep == 0:
                update = soft(field[c, s].astype(F32) + tn_dot(stack, synthesis_ref[...]))
                field_ref[s, span_lanes, :] = update
                analyse(s, update.astype(BF16))
            elif c < chunks - 1:
                field_ref[s, span_lanes, :] = soft(field_ref[s, span_lanes, :] + tn_dot(stack, synthesis_ref[...]))
            else:
                last_ref[s] = stack
            return carry

        low_end = min(RADIUS, local_src)
        high_end = max(local_src - RADIUS, low_end)
        lax.fori_loop(low_end, high_end, source, 0, unroll=4)
        for side in range(2):

            @pl.when(gets[side])
            def _():
                rim(place, side).wait_recv()
                at = 0 if side == 0 else RADIUS + local_src
                near[at : at + RADIUS] = rim_in[place, side].astype(F32)

        lax.fori_loop(0, low_end, source, 0, unroll=4)
        lax.fori_loop(high_end, local_src, source, 0, unroll=4)
        if sweep == 0:
            ship(1, c)

    tables[0].wait()
    for c in range(chunks):
        load(c).wait()

        def source(s, carry):
            analyse(s, field[c, s])
            return carry

        lax.fori_loop(0, local_src, source, 0, unroll=4)
        ship(0, c)
    for table in tables[1:]:
        table.wait()
    build_operator(block_ref, multiples_ref, inner, local_src)
    near[...] = jnp.zeros_like(near)
    for s in range(local_src):
        spans[s] = radius_ref[s : s + 1, :]
    for c in range(chunks):
        own(0, c)
    for c in range(chunks):
        trace_side(0, c)
        if c:
            own(1, c - 1)
    own(1, chunks - 1)
    for c in range(chunks):
        trace_side(1, c)
    for phase in range(4):
        for c in range(chunks):
            await_all(phase, c, back_slabs if phase % 2 else out_slabs, send_sem)
    for place in range(2 * chunks):
        for side in range(2):

            @pl.when(sends[side])
            def _():
                rim(place, side).wait_send()


def finish_kernel(
    once_ref, last_ref, residual_ref, synthesis_hbm, field_hbm, residual_hbm,
    done, synthesis_ref, ready_sem, done_sem, residual_sem, table_sem,
):
    local_src, receivers, _ = once_ref.shape
    width = last_ref.shape[2]
    start = receivers - width
    ready = pltpu.make_async_copy(once_ref.at[:, pl.ds(0, start), :], field_hbm.at[:, pl.ds(0, start), :], ready_sem)
    residual = pltpu.make_async_copy(residual_ref, residual_hbm, residual_sem)
    table = pltpu.make_async_copy(synthesis_hbm, synthesis_ref, table_sem)
    table.start()
    if start:
        ready.start()
    residual.start()
    table.wait()

    def source(s, carry):
        done[s] = soft(once_ref[s, pl.ds(start, width), :] + tn_dot(last_ref[s], synthesis_ref[...]))
        pltpu.make_async_copy(done.at[s], field_hbm.at[s, pl.ds(start, width), :], done_sem).start()
        return carry

    lax.fori_loop(0, local_src, source, 0, unroll=4)
    pltpu.make_async_copy(done, field_hbm.at[:, pl.ds(start, width), :], done_sem).wait()
    residual.wait()
    if start:
        ready.wait()


def on_device(devices, start_field, recorded, multiples, block_index, radius):
    local_src, receivers, samples = start_field.shape
    local_freq = recorded.shape[0]
    rows = 2 * local_freq * devices
    width = 128
    chunks = receivers // width
    table = dft_table(local_freq * devices, samples)
    analysis = jnp.concatenate(halves(table.T), axis=0)
    high, low = halves(step_size * table.T)
    synthesis = jnp.concatenate([high, high, low], axis=0)
    vmem = pl.BlockSpec(memory_space=pltpu.VMEM)
    hbm = pl.BlockSpec(memory_space=pltpu.HBM)
    slab = pltpu.VMEM((2 * chunks, devices, local_freq * 2 * local_src, width), BF16)
    rim = pltpu.VMEM((2 * chunks, 2, RADIUS, rows, width), BF16)
    flat = pltpu.VMEM((rows * local_src, width), F32)
    field_shape = jax.ShapeDtypeStruct(start_field.shape, F32)
    residual_shape = jax.ShapeDtypeStruct((local_freq, receivers * NB, 2 * BS), F32)
    once, last, residual = pl.pallas_call(
        functools.partial(sweeps_kernel, devices, chunks, width),
        out_shape=(field_shape, jax.ShapeDtypeStruct((local_src, 3 * rows, width), BF16), residual_shape),
        in_specs=[hbm] * 7,
        out_specs=(vmem, vmem, vmem),
        scratch_shapes=[
            pltpu.VMEM((chunks, local_src, width, samples), BF16),
            flat,
            flat,
            pltpu.VMEM((local_src + 2 * RADIUS, rows, width), F32),
            pltpu.VMEM((local_src, 1, receivers), jnp.int32),
            pltpu.VMEM((width * NB, 2 * BS), F32),
            pltpu.VMEM((local_freq, devices * 2 * local_src, NB * 2 * BS), BF16),
            slab,
            slab,
            slab,
            slab,
            rim,
            rim,
            pltpu.SMEM(block_index.shape, block_index.dtype),
            pltpu.VMEM((local_freq, receivers * NB, 2 * BS), BF16),
            pltpu.VMEM(multiples.shape, BF16),
            pltpu.VMEM(radius.shape, radius.dtype),
            pltpu.VMEM(analysis.shape, BF16),
            pltpu.VMEM(synthesis.shape, BF16),
            pltpu.SemaphoreType.DMA((chunks,)),
            pltpu.SemaphoreType.DMA((4 * chunks,)),
            pltpu.SemaphoreType.DMA((4 * chunks,)),
            pltpu.SemaphoreType.DMA((2 * chunks, 2)),
            pltpu.SemaphoreType.DMA((2 * chunks, 2)),
            pltpu.SemaphoreType.DMA((6,)),
        ],
        compiler_params=pltpu.CompilerParams(
            collective_id=0, has_side_effects=True, vmem_limit_bytes=28 << 20
        ),
    )(
        *(
            pltpu.with_memory_space_constraint(value, pltpu.HBM)
            for value in (
                block_index, start_field, recorded.reshape(local_freq, receivers * NB, 2 * BS), multiples, radius,
                analysis, synthesis,
            )
        )
    )
    field, residual = pl.pallas_call(
        finish_kernel,
        out_shape=(field_shape, residual_shape),
        in_specs=[vmem] * 3 + [hbm],
        out_specs=(hbm, hbm),
        scratch_shapes=[
            pltpu.VMEM((local_src, width, samples), F32),
            pltpu.VMEM(synthesis.shape, BF16),
            pltpu.SemaphoreType.DMA,
            pltpu.SemaphoreType.DMA,
            pltpu.SemaphoreType.DMA,
            pltpu.SemaphoreType.DMA,
        ],
        compiler_params=pltpu.CompilerParams(vmem_limit_bytes=12 << 20),
    )(once, last, residual, pltpu.with_memory_space_constraint(synthesis, pltpu.HBM))
    return field, residual.reshape(recorded.shape)


def solution(mesh):
    placed = (
        P(("grp", "freq"), None, None),
        P(("grp", "freq"), None, None, None),
        P(("grp", "freq"), None, None, None, None),
        P(),
        P(("grp", "freq"), None),
    )
    return jax.shard_map(
        functools.partial(on_device, mesh.shape["freq"]),
        mesh=mesh,
        in_specs=placed,
        out_specs=(P(("grp", "freq"), None, None), P(("grp", "freq"), None, None, None)),
        check_vma=False,
    )
```

profile of v0, /device:TPU:8, one launch (start us, length us, event | category | flops | bytes accessed | tf_op | source)
XLA Modules:
  0.0 60.2 jit_solution(15470580130187266805)
XLA Ops:
  0.6 54.6 %shard_map.86 = (f32[16,384,512]{2,1,0:T(8,128)S(1)}, bf16[16,96,128]{2,1,0:T(8,128)(2,1)S(1)}, f32[1,1536,128]{2,1,0:T(8,128)S(1)}) custom-call(s32[4,3]{1,0:T(4,128)} %block_hbm.1, bf16[16,384,512]{2,1,0:T(8,128)(2,1)} %start_hbm.1, bf16[1,1536,128]{2,1,0:T(8,128)(2,1)} %bitcast.2, bf16[1,4,3,64,128]{4,3,2,1,0:T(8,128)(2,1)} %multiples_hbm.1, ...), custom_call_target="tpu_custom_call" | custom-call | tf_op jit(solution)/shard_map/pallas_call | solution.py:311
  55.3 4.9 %shard_map.87 = (f32[16,384,512]{2,1,0:T(8,128)}, f32[1,1536,128]{2,1,0:T(8,128)}) custom-call(f32[16,384,512]{2,1,0:T(8,128)S(1)} %get-tuple-element.7.once_ref, bf16[16,96,128]{2,1,0:T(8,128)(2,1)S(1)} %get-tuple-element.8.last_ref, f32[1,1536,128]{2,1,0:T(8,128)S(1)} %get-tuple-element.9.residual_ref, bf16[96,512]{1,0:T(8,128)(2,1)} %constant.19.synthesis_hbm), custom_call_target="tpu_custom_call" | custom-call | tf_op jit(solution)/shard_map/pallas_call | solution.py:355
where the time goes:
time: 60.3 us; the launch traced here: 60.2 us
  Pallas kernels  59.5 us (99%)
  between operations  0.64 us (1%)
    pallas_call x1, Pallas kernels, on_device(): pl.pallas_call(functools.partial(sweeps_kernel, devices, chunks, width),...  54.6 us
    pallas_call x1, Pallas kernels, on_device(): pl.pallas_call(finish_kernel, out_shape=(field_shape, residual_shape), in...  4.92 us

commit v1 on v0

--- a/solution.py
+++ b/solution.py
@@ -13,6 +13,7 @@
 BS = 64
 BANDS = 3
 RADIUS = 4
+PAD = 8
 
 step_size = 0.5
 shrinkage = 0.05
@@ -68,14 +69,16 @@
     devices, chunks, width,
     block_hbm, start_hbm, recorded_hbm, multiples_hbm, radius_hbm, analysis_hbm, synthesis_hbm,
     field_ref, last_ref, residual_ref,
-    field, wide, flat, near, spans, given, inner, out_slabs, in_slabs, back_slabs, edge_slabs, rim_out, rim_in,
+    field, wide, flat, near, radii, spans, shares, given, inner, out_slabs, in_slabs, back_slabs, edge_slabs,
     block_ref, recorded_ref, multiples_ref, radius_ref, analysis_ref, synthesis_ref,
-    load_sem, send_sem, recv_sem, rim_send, rim_recv, table_sem,
+    load_sem, send_sem, recv_sem, table_sem, radii_send, radii_recv,
 ):
     me = lax.axis_index("freq")
     local_src = start_hbm.shape[0]
     local_freq = multiples_hbm.shape[0]
     rows = analysis_ref.shape[0] // 2
+    per = max(1, 8 // local_src)
+    block = per * local_src
     block_cols = 2 * BS
 
     def load(c):
@@ -129,18 +132,33 @@
         whole = refs.at[(phase // 2) * chunks + c, pl.ds(0, devices - 1)]
         pltpu.make_async_copy(whole, whole, sems.at[phase * chunks + c]).wait()
 
-    def rim(place, side):
+    side = radii.shape[0]
+    planes = devices // side
+    plane, spot = me // side, lax.rem(me, side)
+
+    def radii_across(step):
         return pltpu.make_async_remote_copy(
-            src_ref=rim_out.at[place, side],
-            dst_ref=rim_in.at[place, side],
-            send_sem=rim_send.at[place, side],
-            recv_sem=rim_recv.at[place, side],
-            device_id={"freq": lax.rem(me + (1 if side == 0 else devices - 1), devices)},
+            src_ref=radii.at[spot, plane],
+            dst_ref=radii.at[spot, plane],
+            send_sem=radii_send.at[0],
+            recv_sem=radii_recv.at[0],
+            device_id={"freq": lax.rem(plane + step, planes) * side + spot},
             device_id_type=pl.DeviceIdType.MESH,
         )
 
-    sends = (me < devices - 1, me > 0)
-    gets = (me > 0, me < devices - 1)
+    def radii_around(step):
+        return pltpu.make_async_remote_copy(
+            src_ref=radii.at[spot],
+            dst_ref=radii.at[spot],
+            send_sem=radii_send.at[1],
+            recv_sem=radii_recv.at[1],
+            device_id={"freq": plane * side + lax.rem(spot + step, side)},
+            device_id_type=pl.DeviceIdType.MESH,
+        )
+
+    def await_radii(stage, sems):
+        several = radii.at[0, pl.ds(0, planes - 1)] if stage == 0 else radii.at[pl.ds(0, side - 1)]
+        pltpu.make_async_copy(several, several, sems.at[stage]).wait()
 
     def analyse(s, samples):
         both = nt_dot(analysis_ref[...], samples)
@@ -150,13 +168,17 @@
         slabs = wide[...].reshape(devices, local_freq * 2 * local_src, width)
         out_slabs[sweep * chunks + c] = slabs.astype(BF16)
         if sweep == 0 and c == 0:
+            tables[3].wait()
+            radii[spot, plane] = radius_ref[...].astype(F32).astype(BF16)
             pl.semaphore_wait(barrier, devices - 1)
+            for step in range(1, planes):
+                radii_across(step).start()
         exchange(2 * sweep, c, out_slabs, in_slabs)
 
     def own(sweep, c):
         await_all(2 * sweep, c, in_slabs, recv_sem)
         arrived = in_slabs[sweep * chunks + c].astype(F32)
-        backs = []
+        span_lanes = pl.ds(c * width, width)
         for f in range(local_freq):
             part = arrived[:, f * 2 * local_src : (f + 1) * 2 * local_src]
             owned = part.reshape(devices * 2 * local_src, width).T.astype(BF16)
@@ -169,61 +191,67 @@
                     residual_ref[f, pl.ds(c * width * NB + j, width, stride=NB), :] = left
                 narrow.append(left.astype(BF16))
             back = nt_dot(inner[f], jnp.concatenate(narrow, axis=1))
-            backs.append(back.reshape(devices, 2 * local_src, width))
-        back = backs[0] if local_freq == 1 else jnp.concatenate(backs, axis=1)
-        back_slabs[sweep * chunks + c] = back.astype(BF16)
+            for p in range(devices):
+                for h in range(2):
+                    at = (2 * p + h) * local_src
+                    near[h, PAD + p * local_src : PAD + (p + 1) * local_src, :] = back[at : at + local_src]
+            if sweep == 0 and c == 0 and f == 0:
+                gather_spans()
+
+            def smooth(g, carry):
+                start = pl.multiple_of(g * block, 8)
+                rows_of = pl.ds(start, block)
+                span, share = spans[rows_of, span_lanes], shares[rows_of, span_lanes]
+                pair = []
+                for h in range(2):
+                    box = near[h, pl.ds(start + PAD, block), :]
+                    smoothed = box
+                    for offset in range(1, RADIUS + 1):
+                        box = box + (
+                            near[h, pl.ds(start + PAD + offset, block), :]
+                            + near[h, pl.ds(start + PAD - offset, block), :]
+                        )
+                        smoothed = jnp.where(span >= offset, box, smoothed)
+                    pair.append(smoothed * share)
+                for n in range(per):
+                    slab = jnp.concatenate([half[n * local_src : (n + 1) * local_src] for half in pair], axis=0)
+                    part = slice(f * 2 * local_src, (f + 1) * 2 * local_src)
+                    back_slabs[sweep * chunks + c, g * per + n, part, :] = slab.astype(BF16)
+                return carry
+
+            lax.fori_loop(0, devices // per, smooth, 0, unroll=4)
         exchange(2 * sweep + 1, c, back_slabs, edge_slabs)
+
+    def gather_spans():
+        if side > 1:
+            await_radii(1, radii_recv)
+        for p in range(devices):
+            at = p * local_src
+            span = radii[p % side, p // side].astype(F32)
+            spans[at : at + local_src, :] = span
+            shares[at : at + local_src, :] = 1.0 / (2.0 * span + 1.0)
 
     def trace_side(sweep, c):
         place = sweep * chunks + c
         await_all(2 * sweep + 1, c, edge_slabs, recv_sem)
+        if sweep == 1 and c == chunks - 1:
+            last_ref[...] = edge_slabs[place]
+            return
         flat[...] = edge_slabs[place].astype(F32).reshape(rows * local_src, width)
-        for s in range(local_src):
-            near[RADIUS + s] = flat[pl.ds(s, rows, stride=local_src), :]
-        rim_out[place, 0] = near[local_src : local_src + RADIUS].astype(BF16)
-        rim_out[place, 1] = near[RADIUS : 2 * RADIUS].astype(BF16)
-        for side in range(2):
-
-            @pl.when(sends[side])
-            def _():
-                rim(place, side).start()
-
-        span_lanes = pl.ds(c * width, width)
+        lanes = pl.ds(c * width, width)
 
         def source(s, carry):
-            span = spans[s, :, span_lanes]
-            box = near[s + RADIUS]
-            smoothed = box
-            for offset in range(1, RADIUS + 1):
-                box = box + (near[s + RADIUS + offset] + near[s + RADIUS - offset])
-                smoothed = jnp.where(span >= offset, box, smoothed)
-            smoothed = smoothed * (1.0 / (2.0 * span.astype(F32) + 1.0))
-            high = smoothed.astype(BF16)
-            low = (smoothed - high.astype(F32)).astype(BF16)
-            stack = jnp.concatenate([high, low, high], axis=0)
+            spectrum = flat[pl.ds(s, rows, stride=local_src), :].astype(BF16)
+            step = tn_dot(jnp.concatenate([spectrum, spectrum], axis=0), synthesis_ref[...])
             if sweep == 0:
-                update = soft(field[c, s].astype(F32) + tn_dot(stack, synthesis_ref[...]))
-                field_ref[s, span_lanes, :] = update
+                update = soft(field[c, s].astype(F32) + step)
+                field_ref[s, lanes, :] = update
                 analyse(s, update.astype(BF16))
-            elif c < chunks - 1:
-                field_ref[s, span_lanes, :] = soft(field_ref[s, span_lanes, :] + tn_dot(stack, synthesis_ref[...]))
             else:
-                last_ref[s] = stack
+                field_ref[s, lanes, :] = soft(field_ref[s, lanes, :] + step)
             return carry
 
-        low_end = min(RADIUS, local_src)
-        high_end = max(local_src - RADIUS, low_end)
-        lax.fori_loop(low_end, high_end, source, 0, unroll=4)
-        for side in range(2):
-
-            @pl.when(gets[side])
-            def _():
-                rim(place, side).wait_recv()
-                at = 0 if side == 0 else RADIUS + local_src
-                near[at : at + RADIUS] = rim_in[place, side].astype(F32)
-
-        lax.fori_loop(0, low_end, source, 0, unroll=4)
-        lax.fori_loop(high_end, local_src, source, 0, unroll=4)
+        lax.fori_loop(0, local_src, source, 0, unroll=4)
         if sweep == 0:
             ship(1, c)
 
@@ -237,38 +265,38 @@
 
         lax.fori_loop(0, local_src, source, 0, unroll=4)
         ship(0, c)
-    for table in tables[1:]:
-        table.wait()
+    if planes > 1:
+        await_radii(0, radii_recv)
+    for step in range(1, side):
+        radii_around(step).start()
+    for n, table in enumerate(tables):
+        if n not in (0, 3):
+            table.wait()
     build_operator(block_ref, multiples_ref, inner, local_src)
-    near[...] = jnp.zeros_like(near)
-    for s in range(local_src):
-        spans[s] = radius_ref[s : s + 1, :]
-    for c in range(chunks):
-        own(0, c)
-    for c in range(chunks):
-        trace_side(0, c)
-        if c:
-            own(1, c - 1)
-    own(1, chunks - 1)
-    for c in range(chunks):
-        trace_side(1, c)
+    for h in range(2):
+        near[h, 0:PAD, :] = jnp.zeros((PAD, width), F32)
+        near[h, PAD + devices * local_src :, :] = jnp.zeros((PAD, width), F32)
+    for sweep in range(2):
+        for c in range(chunks):
+            own(sweep, c)
+        for c in range(chunks):
+            trace_side(sweep, c)
     for phase in range(4):
         for c in range(chunks):
             await_all(phase, c, back_slabs if phase % 2 else out_slabs, send_sem)
-    for place in range(2 * chunks):
-        for side in range(2):
-
-            @pl.when(sends[side])
-            def _():
-                rim(place, side).wait_send()
+    if planes > 1:
+        await_radii(0, radii_send)
+    if side > 1:
+        await_radii(1, radii_send)
 
 
 def finish_kernel(
     once_ref, last_ref, residual_ref, synthesis_hbm, field_hbm, residual_hbm,
-    done, synthesis_ref, ready_sem, done_sem, residual_sem, table_sem,
+    done, flat, synthesis_ref, ready_sem, done_sem, residual_sem, table_sem,
 ):
     local_src, receivers, _ = once_ref.shape
     width = last_ref.shape[2]
+    rows = flat.shape[0] // local_src
     start = receivers - width
     ready = pltpu.make_async_copy(once_ref.at[:, pl.ds(0, start), :], field_hbm.at[:, pl.ds(0, start), :], ready_sem)
     residual = pltpu.make_async_copy(residual_ref, residual_hbm, residual_sem)
@@ -277,10 +305,13 @@
     if start:
         ready.start()
     residual.start()
+    flat[...] = last_ref[...].astype(F32).reshape(flat.shape)
     table.wait()
 
     def source(s, carry):
-        done[s] = soft(once_ref[s, pl.ds(start, width), :] + tn_dot(last_ref[s], synthesis_ref[...]))
+        spectrum = flat[pl.ds(s, rows, stride=local_src), :].astype(BF16)
+        step = tn_dot(jnp.concatenate([spectrum, spectrum], axis=0), synthesis_ref[...])
+        done[s] = soft(once_ref[s, pl.ds(start, width), :] + step)
         pltpu.make_async_copy(done.at[s], field_hbm.at[s, pl.ds(start, width), :], done_sem).start()
         return carry
 
@@ -300,33 +331,34 @@
     table = dft_table(local_freq * devices, samples)
     analysis = jnp.concatenate(halves(table.T), axis=0)
     high, low = halves(step_size * table.T)
-    synthesis = jnp.concatenate([high, high, low], axis=0)
+    synthesis = jnp.concatenate([high, low], axis=0)
+    side = math.gcd(devices, 4)
+    sources = devices * local_src
     vmem = pl.BlockSpec(memory_space=pltpu.VMEM)
     hbm = pl.BlockSpec(memory_space=pltpu.HBM)
     slab = pltpu.VMEM((2 * chunks, devices, local_freq * 2 * local_src, width), BF16)
-    rim = pltpu.VMEM((2 * chunks, 2, RADIUS, rows, width), BF16)
     flat = pltpu.VMEM((rows * local_src, width), F32)
     field_shape = jax.ShapeDtypeStruct(start_field.shape, F32)
     residual_shape = jax.ShapeDtypeStruct((local_freq, receivers * NB, 2 * BS), F32)
     once, last, residual = pl.pallas_call(
         functools.partial(sweeps_kernel, devices, chunks, width),
-        out_shape=(field_shape, jax.ShapeDtypeStruct((local_src, 3 * rows, width), BF16), residual_shape),
+        out_shape=(field_shape, jax.ShapeDtypeStruct((devices, local_freq * 2 * local_src, width), BF16), residual_shape),
         in_specs=[hbm] * 7,
         out_specs=(vmem, vmem, vmem),
         scratch_shapes=[
             pltpu.VMEM((chunks, local_src, width, samples), BF16),
             flat,
             flat,
-            pltpu.VMEM((local_src + 2 * RADIUS, rows, width), F32),
-            pltpu.VMEM((local_src, 1, receivers), jnp.int32),
+            pltpu.VMEM((2, sources + 2 * PAD, width), F32),
+            pltpu.VMEM((side, devices // side, local_src, receivers), BF16),
+            pltpu.VMEM((sources, receivers), F32),
+            pltpu.VMEM((sources, receivers), F32),
             pltpu.VMEM((width * NB, 2 * BS), F32),
             pltpu.VMEM((local_freq, devices * 2 * local_src, NB * 2 * BS), BF16),
             slab,
             slab,
             slab,
             slab,
-            rim,
-            rim,
             pltpu.SMEM(block_index.shape, block_index.dtype),
             pltpu.VMEM((local_freq, receivers * NB, 2 * BS), BF16),
             pltpu.VMEM(multiples.shape, BF16),
@@ -336,9 +368,9 @@
             pltpu.SemaphoreType.DMA((chunks,)),
             pltpu.SemaphoreType.DMA((4 * chunks,)),
             pltpu.SemaphoreType.DMA((4 * chunks,)),
-            pltpu.SemaphoreType.DMA((2 * chunks, 2)),
-            pltpu.SemaphoreType.DMA((2 * chunks, 2)),
             pltpu.SemaphoreType.DMA((6,)),
+            pltpu.SemaphoreType.DMA((2,)),
+            pltpu.SemaphoreType.DMA((2,)),
         ],
         compiler_params=pltpu.CompilerParams(
             collective_id=0, has_side_effects=True, vmem_limit_bytes=28 << 20
@@ -359,6 +391,7 @@
         out_specs=(hbm, hbm),
         scratch_shapes=[
             pltpu.VMEM((local_src, width, samples), F32),
+            flat,
             pltpu.VMEM(synthesis.shape, BF16),
             pltpu.SemaphoreType.DMA,
             pltpu.SemaphoreType.DMA,

time: 60.3 us -> 49.4 us (0.82)
  the two profiles are of different devices: /device:TPU:8 before, /device:TPU:0 now
where the time goes in v1:
time: 49.4 us; the launch traced here: 49.2 us
  Pallas kernels  48.6 us (98%)
  between operations  0.64 us (1%)
    pallas_call x1, Pallas kernels, on_device(): pl.pallas_call(functools.partial(sweeps_kernel, devices, chunks, width),...  43.6 us
    pallas_call x1, Pallas kernels, on_device(): pl.pallas_call(finish_kernel, out_shape=(field_shape, residual_shape), in...  4.94 us

profile of v1, /device:TPU:0, one launch (start us, length us, event | category | flops | bytes accessed | tf_op | source)
XLA Modules:
  0.0 49.2 jit_solution(1188376426893590354)
XLA Ops:
  0.6 43.6 %shard_map.86 = (f32[16,384,512]{2,1,0:T(8,128)S(1)}, bf16[16,32,128]{2,1,0:T(8,128)(2,1)S(1)}, f32[1,1536,128]{2,1,0:T(8,128)S(1)}) custom-call(s32[4,3]{1,0:T(4,128)} %block_hbm.1, bf16[16,384,512]{2,1,0:T(8,128)(2,1)} %start_hbm.1, bf16[1,1536,128]{2,1,0:T(8,128)(2,1)} %bitcast.2, bf16[1,4,3,64,128]{4,3,2,1,0:T(8,128)(2,1)} %multiples_hbm.1, ...), custom_call_target="tpu_custom_call" | custom-call | tf_op jit(solution)/shard_map/pallas_call | solution.py:343
  44.3 4.9 %shard_map.87 = (f32[16,384,512]{2,1,0:T(8,128)}, f32[1,1536,128]{2,1,0:T(8,128)}) custom-call(f32[16,384,512]{2,1,0:T(8,128)S(1)} %get-tuple-element.7.once_ref, bf16[16,32,128]{2,1,0:T(8,128)(2,1)S(1)} %get-tuple-element.8.last_ref, f32[1,1536,128]{2,1,0:T(8,128)S(1)} %get-tuple-element.9.residual_ref, bf16[64,512]{1,0:T(8,128)(2,1)} %constant.19.synthesis_hbm), custom_call_target="tpu_custom_call" | custom-call | tf_op jit(solution)/shard_map/pallas_call | solution.py:387

commit v2 on v1

--- a/solution.py
+++ b/solution.py
@@ -74,7 +74,7 @@
     load_sem, send_sem, recv_sem, table_sem, radii_send, radii_recv,
 ):
     me = lax.axis_index("freq")
-    local_src = start_hbm.shape[0]
+    local_src, _, samples = start_hbm.shape
     local_freq = multiples_hbm.shape[0]
     rows = analysis_ref.shape[0] // 2
     per = max(1, 8 // local_src)
@@ -160,9 +160,13 @@
         several = radii.at[0, pl.ds(0, planes - 1)] if stage == 0 else radii.at[pl.ds(0, side - 1)]
         pltpu.make_async_copy(several, several, sems.at[stage]).wait()
 
+    pack = math.gcd(local_src, 2)
+
     def analyse(s, samples):
         both = nt_dot(analysis_ref[...], samples)
-        wide[pl.ds(s, rows, stride=local_src), :] = both[:rows] + both[rows:]
+        both = both[:rows] + both[rows:]
+        for n in range(pack):
+            wide[pl.ds(s + n, rows, stride=local_src), :] = both[:, n * width : (n + 1) * width]
 
     def ship(sweep, c):
         slabs = wide[...].reshape(devices, local_freq * 2 * local_src, width)
@@ -240,18 +244,23 @@
         flat[...] = edge_slabs[place].astype(F32).reshape(rows * local_src, width)
         lanes = pl.ds(c * width, width)
 
-        def source(s, carry):
-            spectrum = flat[pl.ds(s, rows, stride=local_src), :].astype(BF16)
-            step = tn_dot(jnp.concatenate([spectrum, spectrum], axis=0), synthesis_ref[...])
+        def source(g, carry):
+            updates = []
+            for n in range(pack):
+                s = g * pack + n
+                spectrum = flat[pl.ds(s, rows, stride=local_src), :].astype(BF16)
+                step = tn_dot(jnp.concatenate([spectrum, spectrum], axis=0), synthesis_ref[...])
+                if sweep == 0:
+                    update = soft(field[c, s].astype(F32) + step)
+                    field_ref[s, lanes, :] = update
+                    updates.append(update.astype(BF16))
+                else:
+                    field_ref[s, lanes, :] = soft(field_ref[s, lanes, :] + step)
             if sweep == 0:
-                update = soft(field[c, s].astype(F32) + step)
-                field_ref[s, lanes, :] = update
-                analyse(s, update.astype(BF16))
-            else:
-                field_ref[s, lanes, :] = soft(field_ref[s, lanes, :] + step)
+                analyse(g * pack, jnp.concatenate(updates, axis=0))
             return carry
 
-        lax.fori_loop(0, local_src, source, 0, unroll=4)
+        lax.fori_loop(0, local_src // pack, source, 0, unroll=4 // pack)
         if sweep == 0:
             ship(1, c)
 
@@ -259,16 +268,17 @@
     for c in range(chunks):
         load(c).wait()
 
-        def source(s, carry):
-            analyse(s, field[c, s])
+        def source(g, carry):
+            analyse(g * pack, field[c, pl.ds(g * pack, pack)].reshape(pack * width, samples))
             return carry
 
-        lax.fori_loop(0, local_src, source, 0, unroll=4)
+        lax.fori_loop(0, local_src // pack, source, 0, unroll=4 // pack)
+        if c == chunks - 1:
+            if planes > 1:
+                await_radii(0, radii_recv)
+            for step in range(1, side):
+                radii_around(step).start()
         ship(0, c)
-    if planes > 1:
-        await_radii(0, radii_recv)
-    for step in range(1, side):
-        radii_around(step).start()
     for n, table in enumerate(tables):
         if n not in (0, 3):
             table.wait()
@@ -303,7 +313,14 @@
     table = pltpu.make_async_copy(synthesis_hbm, synthesis_ref, table_sem)
     table.start()
     if start:
-        ready.start()
+
+        def early(s, carry):
+            pltpu.make_async_copy(
+                once_ref.at[s, pl.ds(0, start), :], field_hbm.at[s, pl.ds(0, start), :], ready_sem
+            ).start()
+            return carry
+
+        lax.fori_loop(0, local_src, early, 0)
     residual.start()
     flat[...] = last_ref[...].astype(F32).reshape(flat.shape)
     table.wait()
@@ -332,7 +349,7 @@
     analysis = jnp.concatenate(halves(table.T), axis=0)
     high, low = halves(step_size * table.T)
     synthesis = jnp.concatenate([high, low], axis=0)
-    side = math.gcd(devices, 4)
+    side = math.gcd(devices, 8)
     sources = devices * local_src
     vmem = pl.BlockSpec(memory_space=pltpu.VMEM)
     hbm = pl.BlockSpec(memory_space=pltpu.HBM)

time: 49.4 us -> 48.8 us (0.988)
  Pallas kernels: 48.6 us -> 48 us
where the time goes in v2:
time: 48.8 us; the launch traced here: 48.6 us
  Pallas kernels  48 us (98%)
  between operations  0.64 us (1%)
    pallas_call x1, Pallas kernels, on_device(): pl.pallas_call(functools.partial(sweeps_kernel, devices, chunks, width),...  43.2 us
    pallas_call x1, Pallas kernels, on_device(): pl.pallas_call(finish_kernel, out_shape=(field_shape, residual_shape), in...  4.8 us

profile of v2, /device:TPU:0, one launch (start us, length us, event | category | flops | bytes accessed | tf_op | source)
XLA Modules:
  0.0 48.6 jit_solution(4386907924952898933)
XLA Ops:
  0.6 43.2 %shard_map.86 = (f32[16,384,512]{2,1,0:T(8,128)S(1)}, bf16[16,32,128]{2,1,0:T(8,128)(2,1)S(1)}, f32[1,1536,128]{2,1,0:T(8,128)S(1)}) custom-call(s32[4,3]{1,0:T(4,128)} %block_hbm.1, bf16[16,384,512]{2,1,0:T(8,128)(2,1)} %start_hbm.1, bf16[1,1536,128]{2,1,0:T(8,128)(2,1)} %bitcast.2, bf16[1,4,3,64,128]{4,3,2,1,0:T(8,128)(2,1)} %multiples_hbm.1, ...), custom_call_target="tpu_custom_call" | custom-call | tf_op jit(solution)/shard_map/pallas_call | solution.py:360
  43.8 4.8 %shard_map.87 = (f32[16,384,512]{2,1,0:T(8,128)}, f32[1,1536,128]{2,1,0:T(8,128)}) custom-call(f32[16,384,512]{2,1,0:T(8,128)S(1)} %get-tuple-element.7.once_ref, bf16[16,32,128]{2,1,0:T(8,128)(2,1)S(1)} %get-tuple-element.8.last_ref, f32[1,1536,128]{2,1,0:T(8,128)S(1)} %get-tuple-element.9.residual_ref, bf16[64,512]{1,0:T(8,128)(2,1)} %constant.19.synthesis_hbm), custom_call_target="tpu_custom_call" | custom-call | tf_op jit(solution)/shard_map/pallas_call | solution.py:404

commit v3 on v2

--- a/solution.py
+++ b/solution.py
@@ -114,51 +114,56 @@
         place = (phase // 2) * chunks + c
 
         def send(step, carry):
-            peer = lax.rem(me + step, devices)
+            peer = step + (step >= me).astype(jnp.int32)
             pltpu.make_async_remote_copy(
                 src_ref=sources.at[place, peer],
                 dst_ref=targets.at[place, me],
-                send_sem=send_sem.at[slot],
+                send_sem=send_sem.at[phase % 2],
                 recv_sem=recv_sem.at[slot],
                 device_id={"freq": peer},
                 device_id_type=pl.DeviceIdType.MESH,
             ).start()
             return carry
 
-        lax.fori_loop(1, devices, send, 0)
+        lax.fori_loop(0, devices - 1, send, 0)
         targets[place, me] = sources[place, me]
 
-    def await_all(phase, c, refs, sems):
+    def await_all(phase, c, refs):
         whole = refs.at[(phase // 2) * chunks + c, pl.ds(0, devices - 1)]
-        pltpu.make_async_copy(whole, whole, sems.at[phase * chunks + c]).wait()
-
-    side = radii.shape[0]
+        pltpu.make_async_copy(whole, whole, recv_sem.at[phase * chunks + c]).wait()
+
+    side = radii.shape[1]
     planes = devices // side
     plane, spot = me // side, lax.rem(me, side)
 
     def radii_across(step):
         return pltpu.make_async_remote_copy(
-            src_ref=radii.at[spot, plane],
-            dst_ref=radii.at[spot, plane],
+            src_ref=radii.at[:, spot, plane],
+            dst_ref=radii.at[:, spot, plane],
             send_sem=radii_send.at[0],
-            recv_sem=radii_recv.at[0],
+            recv_sem=radii_recv.at[chunks],
             device_id={"freq": lax.rem(plane + step, planes) * side + spot},
             device_id_type=pl.DeviceIdType.MESH,
         )
 
-    def radii_around(step):
+    def radii_around(c, step):
         return pltpu.make_async_remote_copy(
-            src_ref=radii.at[spot],
-            dst_ref=radii.at[spot],
+            src_ref=radii.at[c, spot],
+            dst_ref=radii.at[c, spot],
             send_sem=radii_send.at[1],
-            recv_sem=radii_recv.at[1],
+            recv_sem=radii_recv.at[c],
             device_id={"freq": plane * side + lax.rem(spot + step, side)},
             device_id_type=pl.DeviceIdType.MESH,
         )
 
-    def await_radii(stage, sems):
-        several = radii.at[0, pl.ds(0, planes - 1)] if stage == 0 else radii.at[pl.ds(0, side - 1)]
-        pltpu.make_async_copy(several, several, sems.at[stage]).wait()
+    def await_across(sem):
+        if planes > 1:
+            several = radii.at[:, 0, pl.ds(0, planes - 1)]
+            pltpu.make_async_copy(several, several, sem).wait()
+
+    def pass_around(c):
+        for step in range(1, side):
+            radii_around(c, step).start()
 
     pack = math.gcd(local_src, 2)
 
@@ -173,14 +178,16 @@
         out_slabs[sweep * chunks + c] = slabs.astype(BF16)
         if sweep == 0 and c == 0:
             tables[3].wait()
-            radii[spot, plane] = radius_ref[...].astype(F32).astype(BF16)
+            mine = radius_ref[...].astype(F32).astype(BF16)
+            for n in range(chunks):
+                radii[n, spot, plane] = mine[:, n * width : (n + 1) * width]
             pl.semaphore_wait(barrier, devices - 1)
             for step in range(1, planes):
                 radii_across(step).start()
         exchange(2 * sweep, c, out_slabs, in_slabs)
 
     def own(sweep, c):
-        await_all(2 * sweep, c, in_slabs, recv_sem)
+        await_all(2 * sweep, c, in_slabs)
         arrived = in_slabs[sweep * chunks + c].astype(F32)
         span_lanes = pl.ds(c * width, width)
         for f in range(local_freq):
@@ -199,8 +206,8 @@
                 for h in range(2):
                     at = (2 * p + h) * local_src
                     near[h, PAD + p * local_src : PAD + (p + 1) * local_src, :] = back[at : at + local_src]
-            if sweep == 0 and c == 0 and f == 0:
-                gather_spans()
+            if sweep == 0 and f == 0:
+                gather_spans(c)
 
             def smooth(g, carry):
                 start = pl.multiple_of(g * block, 8)
@@ -225,19 +232,22 @@
 
             lax.fori_loop(0, devices // per, smooth, 0, unroll=4)
         exchange(2 * sweep + 1, c, back_slabs, edge_slabs)
-
-    def gather_spans():
+        if sweep == 0 and c + 2 < chunks:
+            pass_around(c + 2)
+
+    def gather_spans(c):
         if side > 1:
-            await_radii(1, radii_recv)
+            several = radii.at[c, pl.ds(0, side - 1)]
+            pltpu.make_async_copy(several, several, radii_recv.at[c]).wait()
         for p in range(devices):
             at = p * local_src
-            span = radii[p % side, p // side].astype(F32)
-            spans[at : at + local_src, :] = span
-            shares[at : at + local_src, :] = 1.0 / (2.0 * span + 1.0)
+            span = radii[c, p % side, p // side].astype(F32)
+            spans[at : at + local_src, c * width : (c + 1) * width] = span
+            shares[at : at + local_src, c * width : (c + 1) * width] = 1.0 / (2.0 * span + 1.0)
 
     def trace_side(sweep, c):
         place = sweep * chunks + c
-        await_all(2 * sweep + 1, c, edge_slabs, recv_sem)
+        await_all(2 * sweep + 1, c, edge_slabs)
         if sweep == 1 and c == chunks - 1:
             last_ref[...] = edge_slabs[place]
             return
@@ -273,12 +283,13 @@
             return carry
 
         lax.fori_loop(0, local_src // pack, source, 0, unroll=4 // pack)
-        if c == chunks - 1:
-            if planes > 1:
-                await_radii(0, radii_recv)
-            for step in range(1, side):
-                radii_around(step).start()
+        if c == min(1, chunks - 1):
+            await_across(radii_recv.at[chunks])
+        if c == min(1, chunks - 1):
+            pass_around(0)
         ship(0, c)
+    if chunks > 1:
+        pass_around(1)
     for n, table in enumerate(tables):
         if n not in (0, 3):
             table.wait()
@@ -291,13 +302,13 @@
             own(sweep, c)
         for c in range(chunks):
             trace_side(sweep, c)
-    for phase in range(4):
-        for c in range(chunks):
-            await_all(phase, c, back_slabs if phase % 2 else out_slabs, send_sem)
-    if planes > 1:
-        await_radii(0, radii_send)
+    for n, slabs in enumerate((out_slabs, back_slabs)):
+        sent = slabs.at[:, pl.ds(0, devices - 1)]
+        pltpu.make_async_copy(sent, sent, send_sem.at[n]).wait()
+    await_across(radii_send.at[0])
     if side > 1:
-        await_radii(1, radii_send)
+        sent = radii.at[:, pl.ds(0, side - 1)]
+        pltpu.make_async_copy(sent, sent, radii_send.at[1]).wait()
 
 
 def finish_kernel(
@@ -367,7 +378,7 @@
             flat,
             flat,
             pltpu.VMEM((2, sources + 2 * PAD, width), F32),
-            pltpu.VMEM((side, devices // side, local_src, receivers), BF16),
+            pltpu.VMEM((chunks, side, devices // side, local_src, width), BF16),
             pltpu.VMEM((sources, receivers), F32),
             pltpu.VMEM((sources, receivers), F32),
             pltpu.VMEM((width * NB, 2 * BS), F32),
@@ -383,11 +394,11 @@
             pltpu.VMEM(analysis.shape, BF16),
             pltpu.VMEM(synthesis.shape, BF16),
             pltpu.SemaphoreType.DMA((chunks,)),
-            pltpu.SemaphoreType.DMA((4 * chunks,)),
+            pltpu.SemaphoreType.DMA((2,)),
             pltpu.SemaphoreType.DMA((4 * chunks,)),
             pltpu.SemaphoreType.DMA((6,)),
             pltpu.SemaphoreType.DMA((2,)),
-            pltpu.SemaphoreType.DMA((2,)),
+            pltpu.SemaphoreType.DMA((chunks + 1,)),
         ],
         compiler_params=pltpu.CompilerParams(
             collective_id=0, has_side_effects=True, vmem_limit_bytes=28 << 20

time: 48.8 us -> 48 us (0.984)
  Pallas kernels: 48 us -> 47.2 us
    pallas_call x1, Pallas kernels: 43.2 us -> 42.4 us  [on_device(): pl.pallas_call(functools.partial(sweeps_kernel, devices, chunks, width),...]
where the time goes in v3:
time: 48 us; the launch traced here: 47.8 us
  Pallas kernels  47.2 us (98%)
  between operations  0.64 us (1%)
    pallas_call x1, Pallas kernels, on_device(): pl.pallas_call(functools.partial(sweeps_kernel, devices, chunks, width),...  42.4 us
    pallas_call x1, Pallas kernels, on_device(): pl.pallas_call(finish_kernel, out_shape=(field_shape, residual_shape), in...  4.8 us

profile of v3, /device:TPU:0, one launch (start us, length us, event | category | flops | bytes accessed | tf_op | source)
XLA Modules:
  0.0 47.8 jit_solution(11639277346796252303)
XLA Ops:
  0.6 42.4 %shard_map.86 = (f32[16,384,512]{2,1,0:T(8,128)S(1)}, bf16[16,32,128]{2,1,0:T(8,128)(2,1)S(1)}, f32[1,1536,128]{2,1,0:T(8,128)S(1)}) custom-call(s32[4,3]{1,0:T(4,128)} %block_hbm.1, bf16[16,384,512]{2,1,0:T(8,128)(2,1)} %start_hbm.1, bf16[1,1536,128]{2,1,0:T(8,128)(2,1)} %bitcast.2, bf16[1,4,3,64,128]{4,3,2,1,0:T(8,128)(2,1)} %multiples_hbm.1, ...), custom_call_target="tpu_custom_call" | custom-call | tf_op jit(solution)/shard_map/pallas_call | solution.py:371
  43.0 4.8 %shard_map.87 = (f32[16,384,512]{2,1,0:T(8,128)}, f32[1,1536,128]{2,1,0:T(8,128)}) custom-call(f32[16,384,512]{2,1,0:T(8,128)S(1)} %get-tuple-element.7.once_ref, bf16[16,32,128]{2,1,0:T(8,128)(2,1)S(1)} %get-tuple-element.8.last_ref, f32[1,1536,128]{2,1,0:T(8,128)S(1)} %get-tuple-element.9.residual_ref, bf16[64,512]{1,0:T(8,128)(2,1)} %constant.19.synthesis_hbm), custom_call_target="tpu_custom_call" | custom-call | tf_op jit(solution)/shard_map/pallas_call | solution.py:415

commit v4 on v3

--- a/solution.py
+++ b/solution.py
@@ -84,6 +84,12 @@
     def load(c):
         return pltpu.make_async_copy(start_hbm.at[:, pl.ds(c * width, width), :], field.at[c], load_sem.at[c])
 
+    barrier = pltpu.get_barrier_semaphore()
+    for shift in range(1, devices):
+        pl.semaphore_signal(
+            barrier, inc=1, device_id={"freq": lax.rem(me + shift, devices)}, device_id_type=pl.DeviceIdType.MESH
+        )
+
     load(0).start()
     tables = [
         pltpu.make_async_copy(source, target, table_sem.at[n])
@@ -103,29 +109,25 @@
         load(c).start()
     for table in tables[1:]:
         table.start()
-    barrier = pltpu.get_barrier_semaphore()
-    for shift in range(1, devices):
-        pl.semaphore_signal(
-            barrier, inc=1, device_id={"freq": lax.rem(me + shift, devices)}, device_id_type=pl.DeviceIdType.MESH
+    def send(phase, c, sources, targets, peer):
+        place = (phase // 2) * chunks + c
+        return pltpu.make_async_remote_copy(
+            src_ref=sources.at[place, peer],
+            dst_ref=targets.at[place, me],
+            send_sem=send_sem.at[phase % 2],
+            recv_sem=recv_sem.at[phase * chunks + c],
+            device_id={"freq": peer},
+            device_id_type=pl.DeviceIdType.MESH,
         )
 
     def exchange(phase, c, sources, targets):
-        slot = phase * chunks + c
         place = (phase // 2) * chunks + c
 
-        def send(step, carry):
-            peer = step + (step >= me).astype(jnp.int32)
-            pltpu.make_async_remote_copy(
-                src_ref=sources.at[place, peer],
-                dst_ref=targets.at[place, me],
-                send_sem=send_sem.at[phase % 2],
-                recv_sem=recv_sem.at[slot],
-                device_id={"freq": peer},
-                device_id_type=pl.DeviceIdType.MESH,
-            ).start()
+        def step(n, carry):
+            send(phase, c, sources, targets, n + (n >= me).astype(jnp.int32)).start()
             return carry
 
-        lax.fori_loop(0, devices - 1, send, 0)
+        lax.fori_loop(0, devices - 1, step, 0)
         targets[place, me] = sources[place, me]
 
     def await_all(phase, c, refs):
@@ -228,10 +230,16 @@
                     slab = jnp.concatenate([half[n * local_src : (n + 1) * local_src] for half in pair], axis=0)
                     part = slice(f * 2 * local_src, (f + 1) * 2 * local_src)
                     back_slabs[sweep * chunks + c, g * per + n, part, :] = slab.astype(BF16)
+                    if f == local_freq - 1:
+
+                        @pl.when(g * per + n != me)
+                        def _():
+                            send(2 * sweep + 1, c, back_slabs, edge_slabs, g * per + n).start()
+
                 return carry
 
             lax.fori_loop(0, devices // per, smooth, 0, unroll=4)
-        exchange(2 * sweep + 1, c, back_slabs, edge_slabs)
+        edge_slabs[sweep * chunks + c, me] = back_slabs[sweep * chunks + c, me]
         if sweep == 0 and c + 2 < chunks:
             pass_around(c + 2)
 

time: 48 us -> 47.8 us (level)
  no operation moved by 1% of the time
where the time goes in v4:
time: 47.8 us; the launch traced here: 47.6 us
  Pallas kernels  47 us (98%)
  between operations  0.64 us (1%)
    pallas_call x1, Pallas kernels, on_device(): pl.pallas_call(functools.partial(sweeps_kernel, devices, chunks, width),...  42.2 us
    pallas_call x1, Pallas kernels, on_device(): pl.pallas_call(finish_kernel, out_shape=(field_shape, residual_shape), in...  4.8 us

profile of v4, /device:TPU:0, one launch (start us, length us, event | category | flops | bytes accessed | tf_op | source)
XLA Modules:
  0.0 47.6 jit_solution(5703671755458214957)
XLA Ops:
  0.6 42.2 %shard_map.86 = (f32[16,384,512]{2,1,0:T(8,128)S(1)}, bf16[16,32,128]{2,1,0:T(8,128)(2,1)S(1)}, f32[1,1536,128]{2,1,0:T(8,128)S(1)}) custom-call(s32[4,3]{1,0:T(4,128)} %block_hbm.1, bf16[16,384,512]{2,1,0:T(8,128)(2,1)} %start_hbm.1, bf16[1,1536,128]{2,1,0:T(8,128)(2,1)} %bitcast.2, bf16[1,4,3,64,128]{4,3,2,1,0:T(8,128)(2,1)} %multiples_hbm.1, ...), custom_call_target="tpu_custom_call" | custom-call | tf_op jit(solution)/shard_map/pallas_call | solution.py:379
  42.8 4.8 %shard_map.87 = (f32[16,384,512]{2,1,0:T(8,128)}, f32[1,1536,128]{2,1,0:T(8,128)}) custom-call(f32[16,384,512]{2,1,0:T(8,128)S(1)} %get-tuple-element.7.once_ref, bf16[16,32,128]{2,1,0:T(8,128)(2,1)S(1)} %get-tuple-element.8.last_ref, f32[1,1536,128]{2,1,0:T(8,128)S(1)} %get-tuple-element.9.residual_ref, bf16[64,512]{1,0:T(8,128)(2,1)} %constant.19.synthesis_hbm), custom_call_target="tpu_custom_call" | custom-call | tf_op jit(solution)/shard_map/pallas_call | solution.py:423

commit v5 on v3

--- a/solution.py
+++ b/solution.py
@@ -83,6 +83,12 @@
 
     def load(c):
         return pltpu.make_async_copy(start_hbm.at[:, pl.ds(c * width, width), :], field.at[c], load_sem.at[c])
+
+    barrier = pltpu.get_barrier_semaphore()
+    for shift in range(1, devices):
+        pl.semaphore_signal(
+            barrier, inc=1, device_id={"freq": lax.rem(me + shift, devices)}, device_id_type=pl.DeviceIdType.MESH
+        )
 
     load(0).start()
     tables = [
@@ -103,12 +109,6 @@
         load(c).start()
     for table in tables[1:]:
         table.start()
-    barrier = pltpu.get_barrier_semaphore()
-    for shift in range(1, devices):
-        pl.semaphore_signal(
-            barrier, inc=1, device_id={"freq": lax.rem(me + shift, devices)}, device_id_type=pl.DeviceIdType.MESH
-        )
-
     def exchange(phase, c, sources, targets):
         slot = phase * chunks + c
         place = (phase // 2) * chunks + c
@@ -136,12 +136,13 @@
     planes = devices // side
     plane, spot = me // side, lax.rem(me, side)
 
-    def radii_across(step):
+    def radii_across(part, step):
+        lanes = radii.at[0:1] if part == 0 else radii.at[1:]
         return pltpu.make_async_remote_copy(
-            src_ref=radii.at[:, spot, plane],
-            dst_ref=radii.at[:, spot, plane],
-            send_sem=radii_send.at[0],
-            recv_sem=radii_recv.at[chunks],
+            src_ref=lanes.at[:, spot, plane],
+            dst_ref=lanes.at[:, spot, plane],
+            send_sem=radii_send.at[part],
+            recv_sem=radii_recv.at[chunks + part],
             device_id={"freq": lax.rem(plane + step, planes) * side + spot},
             device_id_type=pl.DeviceIdType.MESH,
         )
@@ -150,15 +151,15 @@
         return pltpu.make_async_remote_copy(
             src_ref=radii.at[c, spot],
             dst_ref=radii.at[c, spot],
-            send_sem=radii_send.at[1],
+            send_sem=radii_send.at[2],
             recv_sem=radii_recv.at[c],
             device_id={"freq": plane * side + lax.rem(spot + step, side)},
             device_id_type=pl.DeviceIdType.MESH,
         )
 
-    def await_across(sem):
-        if planes > 1:
-            several = radii.at[:, 0, pl.ds(0, planes - 1)]
+    def await_across(part, sem):
+        if planes > 1 and (part == 0 or chunks > 1):
+            several = (radii.at[0:1] if part == 0 else radii.at[1:]).at[:, 0, pl.ds(0, planes - 1)]
             pltpu.make_async_copy(several, several, sem).wait()
 
     def pass_around(c):
@@ -183,8 +184,11 @@
                 radii[n, spot, plane] = mine[:, n * width : (n + 1) * width]
             pl.semaphore_wait(barrier, devices - 1)
             for step in range(1, planes):
-                radii_across(step).start()
+                radii_across(0, step).start()
         exchange(2 * sweep, c, out_slabs, in_slabs)
+        if sweep == 0 and c == 0 and chunks > 1:
+            for step in range(1, planes):
+                radii_across(1, step).start()
 
     def own(sweep, c):
         await_all(2 * sweep, c, in_slabs)
@@ -284,10 +288,11 @@
 
         lax.fori_loop(0, local_src // pack, source, 0, unroll=4 // pack)
         if c == min(1, chunks - 1):
-            await_across(radii_recv.at[chunks])
+            await_across(0, radii_recv.at[chunks])
         if c == min(1, chunks - 1):
             pass_around(0)
         ship(0, c)
+    await_across(1, radii_recv.at[chunks + 1])
     if chunks > 1:
         pass_around(1)
     for n, table in enumerate(tables):
@@ -305,10 +310,11 @@
     for n, slabs in enumerate((out_slabs, back_slabs)):
         sent = slabs.at[:, pl.ds(0, devices - 1)]
         pltpu.make_async_copy(sent, sent, send_sem.at[n]).wait()
-    await_across(radii_send.at[0])
+    await_across(0, radii_send.at[0])
+    await_across(1, radii_send.at[1])
     if side > 1:
         sent = radii.at[:, pl.ds(0, side - 1)]
-        pltpu.make_async_copy(sent, sent, radii_send.at[1]).wait()
+        pltpu.make_async_copy(sent, sent, radii_send.at[2]).wait()
 
 
 def finish_kernel(
@@ -397,8 +403,8 @@
             pltpu.SemaphoreType.DMA((2,)),
             pltpu.SemaphoreType.DMA((4 * chunks,)),
             pltpu.SemaphoreType.DMA((6,)),
-            pltpu.SemaphoreType.DMA((2,)),
-            pltpu.SemaphoreType.DMA((chunks + 1,)),
+            pltpu.SemaphoreType.DMA((3,)),
+            pltpu.SemaphoreType.DMA((chunks + 2,)),
         ],
         compiler_params=pltpu.CompilerParams(
             collective_id=0, has_side_effects=True, vmem_limit_bytes=28 << 20

time: 48 us -> 47.9 us (level)
  no operation moved by 1% of the time
where the time goes in v5:
time: 47.9 us; the launch traced here: 47.8 us
  Pallas kernels  47.1 us (98%)
  between operations  0.64 us (1%)
    pallas_call x1, Pallas kernels, on_device(): pl.pallas_call(functools.partial(sweeps_kernel, devices, chunks, width),...  42.3 us
    pallas_call x1, Pallas kernels, on_device(): pl.pallas_call(finish_kernel, out_shape=(field_shape, residual_shape), in...  4.8 us

profile of v5, /device:TPU:0, one launch (start us, length us, event | category | flops | bytes accessed | tf_op | source)
XLA Modules:
  0.0 47.8 jit_solution(9526546253975752998)
XLA Ops:
  0.6 42.3 %shard_map.86 = (f32[16,384,512]{2,1,0:T(8,128)S(1)}, bf16[16,32,128]{2,1,0:T(8,128)(2,1)S(1)}, f32[1,1536,128]{2,1,0:T(8,128)S(1)}) custom-call(s32[4,3]{1,0:T(4,128)} %block_hbm.1, bf16[16,384,512]{2,1,0:T(8,128)(2,1)} %start_hbm.1, bf16[1,1536,128]{2,1,0:T(8,128)(2,1)} %bitcast.2, bf16[1,4,3,64,128]{4,3,2,1,0:T(8,128)(2,1)} %multiples_hbm.1, ...), custom_call_target="tpu_custom_call" | custom-call | tf_op jit(solution)/shard_map/pallas_call | solution.py:377
  43.0 4.8 %shard_map.87 = (f32[16,384,512]{2,1,0:T(8,128)}, f32[1,1536,128]{2,1,0:T(8,128)}) custom-call(f32[16,384,512]{2,1,0:T(8,128)S(1)} %get-tuple-element.7.once_ref, bf16[16,32,128]{2,1,0:T(8,128)(2,1)S(1)} %get-tuple-element.8.last_ref, f32[1,1536,128]{2,1,0:T(8,128)S(1)} %get-tuple-element.9.residual_ref, bf16[64,512]{1,0:T(8,128)(2,1)} %constant.19.synthesis_hbm), custom_call_target="tpu_custom_call" | custom-call | tf_op jit(solution)/shard_map/pallas_call | solution.py:421
